TPU v7x, 256 devices: a whole 4x4x8 slice. The times are simulated.
256 devices in a mesh: dp: 64 (over z, y, core), section: 4 (over x).
Axes of the slice: x: 4, y: 4, z: 8, core: 2. Of those that a mesh axis runs over, the one named last changes fastest.
Arguments:
- hidden_in: bfloat16 [4, 2, 64, 4096], P('section', None, 'dp'), may hold values from -48 to 48
- grad_out: bfloat16 [2, 64, 4096], P(None, 'dp'), may hold values from -6 to 6
- weight_gate: bfloat16 [4, 14336, 4096], P('section', 'dp'), may hold values from -0.09375 to 0.09375
- weight_up: bfloat16 [4, 14336, 4096], P('section', 'dp'), may hold values from -0.09375 to 0.09375
- weight_down: bfloat16 [4, 14336, 4096], P('section', 'dp'), may hold values from -0.046875 to 0.046875
- gain: float32 [4, 4096], P('section'), may hold values from 0.5 to 1.5
- counts: int32 [2], replicated, may hold values from 1 to 64, 85 in all
Outputs:
- grad_inputs: bfloat16 [4, 2, 64, 4096], P('section', None, 'dp')
- gate_grads: bfloat16 [4, 14336, 4096], P('section', 'dp')
- up_grads: bfloat16 [4, 14336, 4096], P('section', 'dp')
- down_grads: bfloat16 [4, 14336, 4096], P('section', 'dp')
- gain_grads: float32 [4, 4096], P('section')
Inputs may be any that keep to these rules, and one draw needn't show every extreme that they name: The 2 counts sum to 85.
All inputs are finite; a program needn't handle non-finite values.
Results may differ from a plain program's by a relative error of at most 0.012.
Values may be sent and summed in bfloat16 or wider, within the bound.
No kernel may reach another device: no remote copies, remote signals or barrier semaphores. Data moves between devices by JAX's collectives and lax.ppermute only.
A program may use at most 128 MiB of HBM per device.

v0:
```python
import jax
import jax.numpy as jnp
from jax import lax
from jax.sharding import PartitionSpec as P


def from_behind(x, axis, by):
    size = lax.axis_size(axis)
    pairs = [(i, i + by) for i in range(size) if 0 <= i + by < size]
    return lax.ppermute(x, axis, pairs)


def norm_rows(layer_rows, gain_row):
    row_values = layer_rows.astype(jnp.float32)
    inv_rms = lax.rsqrt(jnp.mean(row_values * row_values, axis=-1, keepdims=True) + 1e-05)
    normed_rows = (row_values * inv_rms * gain_row).astype(jnp.bfloat16)
    return (inv_rms, normed_rows)


def unit_grads(upstream, gate_pre, up_pre, down_mat):
    sigmoid_pre = jax.nn.sigmoid(gate_pre)
    silu_pre = gate_pre * sigmoid_pre
    activation = (silu_pre * up_pre).astype(jnp.bfloat16)
    grad_act = lax.dot_general(
        upstream, down_mat, (((1,), (1,)), ((), ())), preferred_element_type=jnp.float32
    )
    grad_gate = (grad_act * up_pre * sigmoid_pre * (1.0 + gate_pre * (1.0 - sigmoid_pre))).astype(
        jnp.bfloat16
    )
    grad_up = (grad_act * silu_pre).astype(jnp.bfloat16)
    return (activation, grad_gate, grad_up)


def norm_back(layer_rows, inv_rms, upstream, grad_normed, gain_row):
    row_values = layer_rows.astype(jnp.float32)
    gained_grad = gain_row * grad_normed
    inner_sum = jnp.sum(gained_grad * row_values, axis=-1, keepdims=True)
    feature_count = row_values.shape[-1]
    grad_rows = (
        upstream.astype(jnp.float32)
        + inv_rms * gained_grad
        - row_values * inv_rms**3 * inner_sum / feature_count
    )
    return grad_rows.astype(jnp.bfloat16)


def transposed_product(left_rows, right_rows):
    return lax.dot_general(
        left_rows, right_rows, (((0,), (0,)), ((), ())), preferred_element_type=jnp.float32
    )


def pick_block(stacked, index_value):
    return lax.dynamic_index_in_dim(stacked, index_value, 0, keepdims=False)


def on_device(hidden_in, grad_out, weight_gate, weight_up, weight_down, gain, counts):
    section_count = lax.axis_size("section")
    section_pos = lax.axis_index("section")
    dp_pos = lax.axis_index("dp")
    layer_rows = hidden_in[0]
    gate_mat = weight_gate[0]
    up_mat = weight_up[0]
    down_mat = weight_down[0]
    gain_row = gain[0]
    batch_count, slot_local, feature_count = layer_rows.shape
    unit_count = gate_mat.shape[0]
    full_slots = slot_local * lax.axis_size("dp")
    slot_ids = dp_pos * slot_local + jnp.arange(slot_local)
    live_slots = slot_ids[None, :] < counts[:, None]
    top_local = jnp.where(live_slots[:, :, None], grad_out, jnp.zeros((), jnp.bfloat16))
    is_last = section_pos == section_count - 1
    top_whole = lax.all_gather(top_local, "dp", axis=1, tiled=True)
    received = jnp.zeros((full_slots, feature_count), jnp.bfloat16)
    gathered_all = lax.all_gather(layer_rows, "dp", axis=1, tiled=True)
    all_inv, all_normed = norm_rows(gathered_all, gain_row)
    all_gate = jnp.einsum("mpd,fd->mpf", all_normed, gate_mat, preferred_element_type=jnp.float32)
    all_up = jnp.einsum("mpd,fd->mpf", all_normed, up_mat, preferred_element_type=jnp.float32)
    grad_store = jnp.zeros_like(layer_rows)
    gate_total = jnp.zeros((unit_count, feature_count), jnp.float32)
    up_total = jnp.zeros((unit_count, feature_count), jnp.float32)
    down_total = jnp.zeros((unit_count, feature_count), jnp.float32)
    gain_total = jnp.zeros((feature_count,), jnp.float32)
    last_step = batch_count + section_count - 2
    for step_index in range(batch_count + section_count - 1):
        micro_index = step_index - (section_count - 1 - section_pos)
        is_valid = (micro_index >= 0) & (micro_index < batch_count)
        clamped = jnp.clip(micro_index, 0, batch_count - 1)
        gathered = pick_block(gathered_all, clamped)
        gate_pre = pick_block(all_gate, clamped)
        up_pre = pick_block(all_up, clamped)
        full_inv = pick_block(all_inv, clamped)
        full_normed = pick_block(all_normed, clamped)
        full_up = jnp.where(is_last, pick_block(top_whole, clamped), received)
        full_up = jnp.where(is_valid, full_up, jnp.zeros((), jnp.bfloat16))
        activation, grad_gate, grad_up = unit_grads(full_up, gate_pre, up_pre, down_mat)
        gate_total = gate_total + transposed_product(grad_gate, full_normed)
        up_total = up_total + transposed_product(grad_up, full_normed)
        down_total = down_total + transposed_product(activation, full_up)
        partial_sum = jnp.dot(grad_gate, gate_mat, preferred_element_type=jnp.float32) + jnp.dot(
            grad_up, up_mat, preferred_element_type=jnp.float32
        )
        grad_normed = lax.psum(partial_sum, "dp")
        grad_full = norm_back(gathered, full_inv, full_up, grad_normed, gain_row)
        gain_total = gain_total + jnp.sum(
            grad_normed * gathered.astype(jnp.float32) * full_inv, axis=0
        )
        grad_own = lax.dynamic_slice_in_dim(grad_full, dp_pos * slot_local, slot_local, 0)
        old_rows = pick_block(grad_store, clamped)
        grad_store = lax.dynamic_update_index_in_dim(
            grad_store, jnp.where(is_valid, grad_own, old_rows), clamped, 0
        )
        if step_index < last_step:
            received = from_behind(grad_full, "section", -1)
    return (
        grad_store[None],
        gate_total.astype(jnp.bfloat16)[None],
        up_total.astype(jnp.bfloat16)[None],
        down_total.astype(jnp.bfloat16)[None],
        gain_total[None],
    )


def solution(mesh):
    return jax.shard_map(
        on_device,
        mesh=mesh,
        in_specs=(
            P("section", None, "dp", None),
            P(None, "dp", None),
            P("section", "dp", None),
            P("section", "dp", None),
            P("section", "dp", None),
            P("section", None),
            P(),
        ),
        out_specs=(
            P("section", None, "dp", None),
            P("section", "dp", None),
            P("section", "dp", None),
            P("section", "dp", None),
            P("section", None),
        ),
        check_vma=False,
    )
```

profile of v0, /device:TPU:2, one launch (start us, length us, event | category | flops | bytes accessed | tf_op | source)
XLA Modules:
  0.0 1220.3 jit_solution(14955202066246153748)
XLA Ops:
  10.1 80.4 %all-gather.6.cloned.1.call-done = bf16[1,2,64,4096]{3,1,0,2:T(2,128)(2,1)} async-done(((bf16[1,2,1,4096]{3,1,0,2:T(2,128)(2,1)}), bf16[1,2,64,4096]{3,1,0,2:T(2,128)(2,1)}) %all-gather.6.cloned.1.call-update) | async-done | bytes 1048592 | tf_op jit(solution)/shard_map/all_gather | solution.py:75
  97.3 71.2 %all-gather.4.cloned.1.call-done = bf16[2,64,4096]{2,0,1:T(2,128)(2,1)} async-done(((bf16[2,1,4096]{2,0,1:T(2,128)(2,1)}), bf16[2,64,4096]{2,0,1:T(2,128)(2,1)}) %all-gather.4.cloned.1.call-update) | async-done | bytes 1048592 | tf_op jit(solution)/shard_map/all_gather | solution.py:73
  168.5 9.9 constant_dynamic-slice_fusion.1
  187.0 2.9 fusion.147
  189.8 177.9 %all-reduce.6.cloned.1.call-done = f32[64,4096]{1,0:T(8,128)} async-done(((f32[64,4096]{1,0:T(8,128)}), f32[64,4096]{1,0:T(8,128)}) %all-reduce.6.cloned.1.call-update) | async-done | bytes 1048592 | tf_op jit(solution)/shard_map/psum | solution.py:103
  370.1 2.6 fusion.43
  372.7 2.6 collective-permute-start
  380.2 5.8 collective-permute-done
  393.9 4.5 convolution_add_fusion.5
  398.4 177.5 %all-reduce.8.cloned.1.call-done = f32[64,4096]{1,0:T(8,128)} async-done(((f32[64,4096]{1,0:T(8,128)}), f32[64,4096]{1,0:T(8,128)}) %all-reduce.8.cloned.1.call-update) | async-done | bytes 1048592 | tf_op jit(solution)/shard_map/psum | solution.py:103
  582.5 4.8 convolution_add_fusion.9
  589.8 3.5 collective-permute-done.1
  600.6 4.5 convolution_add_fusion.4
  605.1 178.0 %all-reduce.10.cloned.1.call-done = f32[64,4096]{1,0:T(8,128)} async-done(((f32[64,4096]{1,0:T(8,128)}), f32[64,4096]{1,0:T(8,128)}) %all-reduce.10.cloned.1.call-update) | async-done | bytes 1048592 | tf_op jit(solution)/shard_map/psum | solution.py:103
  790.4 4.6 convolution_add_fusion.8
  798.0 3.5 collective-permute-done.2
  809.1 4.7 convolution_add_fusion.3
  816.3 178.0 %all-reduce.12.cloned.1.call-done = f32[64,4096]{1,0:T(8,128)} async-done(((f32[64,4096]{1,0:T(8,128)}), f32[64,4096]{1,0:T(8,128)}) %all-reduce.12.cloned.1.call-update) | async-done | bytes 1048592 | tf_op jit(solution)/shard_map/psum | solution.py:103
  1006.4 6.3 collective-permute-done.3
  1022.0 4.1 fusion.6
  1026.1 2.8 fusion.7
  1029.0 4.1 fusion.5
  1033.1 174.6 %all-reduce.14.cloned.1.call-done = f32[64,4096]{1,0:T(8,128)} async-done(((f32[64,4096]{1,0:T(8,128)}), f32[64,4096]{1,0:T(8,128)}) %all-reduce.14.cloned.1.call-update) | async-done | bytes 1048592 | tf_op jit(solution)/shard_map/psum | solution.py:103
  1209.8 2.8 fusion.153
  (192 shorter events, 94.1 us)
Async XLA Ops:
  7.2 87.8 %copy-start = (bf16[1,224,4096]{2,1,0:T(8,128)(2,1)S(1)}, bf16[1,224,4096]{2,1,0:T(8,128)(2,1)}, u32[]{:S(2)}) copy-start(bf16[1,224,4096]{2,1,0:T(8,128)(2,1)} %param.9) | copy-start | bytes 5505028
  7.2 83.4 %all-gather.6.cloned.1.call-start = ((), (), s32[]{:S(2)}) async-start(), calls=%async_computation.6 | async-start | bytes 1064960 | tf_op jit(solution)/shard_map/all_gather | solution.py:75
  7.9 160.6 %all-gather.4.cloned.1.call-start = ((), (), s32[]{:S(2)}) async-start(), calls=%async_computation | async-start | bytes 1064960 | tf_op jit(solution)/shard_map/all_gather | solution.py:73
  10.1 357.7 %all-reduce.6.cloned.1.call-start = ((), (), s32[]{:S(2)}) async-start(), calls=%async_computation.1 | async-start | bytes 2097152 | tf_op jit(solution)/shard_map/psum | solution.py:103
  97.3 89.6 %copy-start.29 = (f32[2,64,224]{2,1,0:T(8,128)}, f32[2,64,224]{2,1,0:T(8,128)S(1)}, u32[]{:S(2)}) copy-start(f32[2,64,224]{2,1,0:T(8,128)S(1)} %fusion.23) | copy-start | bytes 344068
  168.5 10.0 copy-start.12
  182.3 393.6 %all-reduce.8.cloned.1.call-start = ((), (), s32[]{:S(2)}) async-start(), calls=%async_computation.2 | async-start | bytes 2097152 | tf_op jit(solution)/shard_map/psum | solution.py:103
  187.0 191.0 %copy-start.58 = (f32[64]{0:T(128)}, f32[64]{0:T(128)S(1)}, u32[]{:S(2)}) copy-start(f32[64]{0:T(128)S(1)} %get-tuple-element.16) | copy-start | bytes 772
  187.0 180.8 %copy-start.35 = (f32[1,4096]{1,0:T(1,128)S(1)}, f32[1,4096]{1,0:T(1,128)}, u32[]{:S(2)}) copy-start(f32[1,4096]{1,0:T(1,128)} %param.12) | copy-start | bytes 49156
  372.7 13.2 %collective-permute-start = (bf16[64,4096]{1,0:T(8,128)(2,1)S(1)}, bf16[64,4096]{1,0:T(8,128)(2,1)S(1)}, u32[]{:S(2)}, u32[]{:S(2)}) collective-permute-start(bf16[64,4096]{1,0:T(8,128)(2,1)S(1)} %fusion.43), channel_id=1, source_target_pairs={{1,0},{2,1},{3,2},{5,4},{6,5},{7,6},{9,8},{10,9},{11,10},{13,12},{... | collective-permute-start | bytes 1572872 | tf_op jit(solution)/shard_map/ppermute | solution.py:10
  390.4 392.7 %all-reduce.10.cloned.1.call-start = ((), (), s32[]{:S(2)}) async-start(), calls=%async_computation.3 | async-start | bytes 2097152 | tf_op jit(solution)/shard_map/psum | solution.py:103
  579.8 13.4 %collective-permute-start.1 = (bf16[64,4096]{1,0:T(8,128)(2,1)S(1)}, bf16[64,4096]{1,0:T(8,128)(2,1)S(1)}, u32[]{:S(2)}, u32[]{:S(2)}) collective-permute-start(bf16[64,4096]{1,0:T(8,128)(2,1)S(1)} %fusion.50), channel_id=1, source_target_pairs={{1,0},{2,1},{3,2},{5,4},{6,5},{7,6},{9,8},{10,9},{11,10},{13,12},{... | collective-permute-start | bytes 1572872 | tf_op jit(solution)/shard_map/ppermute | solution.py:10
  593.9 191.6 %copy-start.23 = (bf16[64,4096]{1,0:T(8,128)(2,1)}, bf16[64,4096]{1,0:T(8,128)(2,1)S(1)}, u32[]{:S(2)}) copy-start(bf16[64,4096]{1,0:T(8,128)(2,1)S(1)} %fusion.73) | copy-start | bytes 1572868
  597.6 396.7 %all-reduce.12.cloned.1.call-start = ((), (), s32[]{:S(2)}) async-start(), calls=%async_computation.4 | async-start | bytes 2097152 | tf_op jit(solution)/shard_map/psum | solution.py:103
  787.8 13.6 %collective-permute-start.2 = (bf16[64,4096]{1,0:T(8,128)(2,1)}, bf16[64,4096]{1,0:T(8,128)(2,1)S(1)}, u32[]{:S(2)}, u32[]{:S(2)}) collective-permute-start(bf16[64,4096]{1,0:T(8,128)(2,1)} %fusion.57), channel_id=1, source_target_pairs={{1,0},{2,1},{3,2},{5,4},{6,5},{7,6},{9,8},{10,9},{11,10},{13,12},{... | collective-permute-start | bytes 1572872 | tf_op jit(solution)/shard_map/ppermute | solution.py:10
  808.8 398.8 %all-reduce.14.cloned.1.call-start = ((), (), s32[]{:S(2)}) async-start(), calls=%async_computation.5 | async-start | bytes 2097152 | tf_op jit(solution)/shard_map/psum | solution.py:103
  999.1 13.7 %collective-permute-start.3 = (bf16[64,4096]{1,0:T(8,128)(2,1)}, bf16[64,4096]{1,0:T(8,128)(2,1)}, u32[]{:S(2)}, u32[]{:S(2)}) collective-permute-start(bf16[64,4096]{1,0:T(8,128)(2,1)} %fusion.64), channel_id=1, source_target_pairs={{1,0},{2,1},{3,2},{5,4},{6,5},{7,6},{9,8},{10,9},{11,10},{13,12},{... | collective-permute-start | bytes 1572872 | tf_op jit(solution)/shard_map/ppermute | solution.py:10
  1006.4 8.4 copy-start.16
  1029.0 178.7 %copy-start.11 = (bf16[1,2,64,4096]{3,2,1,0:T(8,128)(2,1)S(1)}, bf16[1,2,64,4096]{3,2,1,0:T(8,128)(2,1)}, u32[]{:S(2)}) copy-start(bf16[1,2,64,4096]{3,2,1,0:T(8,128)(2,1)} %copy.28) | copy-start | bytes 3145732
  1033.0 176.8 %copy-start.41 = (bf16[2,1,4096]{2,0,1:T(2,128)(2,1)S(1)}, bf16[2,1,4096]{2,0,1:T(2,128)(2,1)}, u32[]{:S(2)}) copy-start(bf16[2,1,4096]{2,0,1:T(2,128)(2,1)} %dynamic_update_slice.20) | copy-start | bytes 49156
  1033.0 179.8 %copy-start.54 = (f32[4096]{0:T(1024)S(1)}, f32[4096]{0:T(1024)}, u32[]{:S(2)}) copy-start(f32[4096]{0:T(1024)} %get-tuple-element.7) | copy-start | bytes 49156
  1033.0 179.8 %copy-start.55 = (f32[4096]{0:T(1024)S(1)}, f32[4096]{0:T(1024)}, u32[]{:S(2)}) copy-start(f32[4096]{0:T(1024)} %get-tuple-element.5) | copy-start | bytes 49156
  1033.0 179.8 %copy-start.56 = (f32[4096]{0:T(1024)S(1)}, f32[4096]{0:T(1024)}, u32[]{:S(2)}) copy-start(f32[4096]{0:T(1024)} %get-tuple-element.9) | copy-start | bytes 49156
  1033.0 179.8 %copy-start.57 = (f32[4096]{0:T(1024)S(1)}, f32[4096]{0:T(1024)}, u32[]{:S(2)}) copy-start(f32[4096]{0:T(1024)} %get-tuple-element.11) | copy-start | bytes 49156
  (46 other events, 166.9 us)
Sparse Core Ops, SparseCore 0:
  10.8 79.7 all-gather.5
  93.9 74.5 all-gather.3
  182.4 185.2 all-reduce.5
  390.5 185.3 all-reduce.7
  597.7 185.3 all-reduce.9
  808.9 185.3 all-reduce.11
  1022.1 185.4 all-reduce.13
where the time goes:
time: 1220 us
  waiting for transfers between devices  1060 us (87%)
  matrix products  68.6 us (6%)
  other arithmetic  42.1 us (3%)
  local copies, waits for them, and re-layouts  26.6 us (2%)
  between operations  14.8 us (1%)
    psum x5, waiting for transfers between devices, on_device(): grad_normed = lax.psum(partial_sum, 'dp')  886 us
    all_gather x1, waiting for transfers between devices, on_device(): gathered_all = lax.all_gather(layer_rows, 'dp', axis=1, tiled=True)  80.4 us
    all_gather x1, waiting for transfers between devices, on_device(): top_whole = lax.all_gather(top_local, 'dp', axis=1, tiled=True)  71.2 us
    dot_general x15, matrix products, transposed_product(): lax.dot_general(left_rows, right_rows, (((0,), (0,)), ((), ())), preferre...  52.1 us
  transfers between devices with their start and end apart: 11, of which 11 were waited for; matrix products, arithmetic and copies ran while one was open for 6% of the time, Pallas kernels for 0%

commit v1 on v0

--- a/solution.py
+++ b/solution.py
@@ -72,7 +72,9 @@
     is_last = section_pos == section_count - 1
     top_whole = lax.all_gather(top_local, "dp", axis=1, tiled=True)
     received = jnp.zeros((full_slots, feature_count), jnp.bfloat16)
-    gathered_all = lax.all_gather(layer_rows, "dp", axis=1, tiled=True)
+    gathered_all = jnp.concatenate(
+        lax.all_to_all(jnp.stack([layer_rows] * lax.axis_size("dp")), "dp", 0, 0), axis=1
+    )
     all_inv, all_normed = norm_rows(gathered_all, gain_row)
     all_gate = jnp.einsum("mpd,fd->mpf", all_normed, gate_mat, preferred_element_type=jnp.float32)
     all_up = jnp.einsum("mpd,fd->mpf", all_normed, up_mat, preferred_element_type=jnp.float32)

time: 1220 us -> 1170 us (0.959)
  waiting for transfers between devices: 1060 us -> 977 us
  starting transfers between devices: 10.9 us -> 23.6 us
    all_gather x1 -> x0, waiting for transfers between devices: 80.4 us -> none  [on_device(): gathered_all = lax.all_gather(layer_rows, 'dp', axis=1, tiled=True)]
    all_to_all x0 -> x1, waiting for transfers between devices: none -> 28.1 us  [on_device(): lax.all_to_all(jnp.stack([layer_rows] * lax.axis_size('dp')), 'dp', 0, 0)]
    all_gather x1, waiting for transfers between devices: 71.2 us -> 47.6 us  [on_device(): top_whole = lax.all_gather(top_local, 'dp', axis=1, tiled=True)]
where the time goes in v1:
time: 1170 us; the launch traced here: 1160 us
  waiting for transfers between devices  977 us (84%)
  matrix products  67 us (6%)
  other arithmetic  44.7 us (4%)
  local copies, waits for them, and re-layouts  35.6 us (3%)
  starting transfers between devices  23.6 us (2%)
  between operations  15 us (1%)
    psum x5, waiting for transfers between devices, on_device(): grad_normed = lax.psum(partial_sum, 'dp')  878 us
    dot_general x15, matrix products, transposed_product(): lax.dot_general(left_rows, right_rows, (((0,), (0,)), ((), ())), preferre...  47.7 us
    all_gather x1, waiting for transfers between devices, on_device(): top_whole = lax.all_gather(top_local, 'dp', axis=1, tiled=True)  47.6 us
    all_to_all x1, waiting for transfers between devices, on_device(): lax.all_to_all(jnp.stack([layer_rows] * lax.axis_size('dp')), 'dp', 0, 0)  28.1 us
  transfers between devices with their start and end apart: 11, of which 11 were waited for; matrix products, arithmetic and copies ran while one was open for 6% of the time, Pallas kernels for 0%

profile of v1, /device:TPU:2, one launch (start us, length us, event | category | flops | bytes accessed | tf_op | source)
XLA Modules:
  0.0 1162.8 jit_solution(13771343250536539774)
XLA Ops:
  10.0 12.1 %all-to-all-start = ((bf16[64,2,1,4096]{3,1,2,0:T(2,128)(2,1)}), bf16[64,2,1,4096]{3,1,2,0:T(2,128)(2,1)S(1)}, u32[]{:S(2)}, u32[]{:S(2)}) async-start(bf16[64,2,1,4096]{3,1,2,0:T(2,128)(2,1)} %stack.3), calls=%async_computation | async-start | bytes 2097152 | tf_op jit(solution)/shard_map/all_to_all | solution.py:76
  23.0 28.1 %all-to-all-done = bf16[64,2,1,4096]{3,1,2,0:T(2,128)(2,1)S(1)} async-done(((bf16[64,2,1,4096]{3,1,2,0:T(2,128)(2,1)}), bf16[64,2,1,4096]{3,1,2,0:T(2,128)(2,1)S(1)}, u32[]{:S(2)}, u32[]{:S(2)}) %all-to-all-start) | async-done | bytes 1048608 | tf_op jit(solution)/shard_map/all_to_all | solution.py:76
  56.8 47.6 %all-gather.2.cloned.1.call-done = bf16[2,64,4096]{2,0,1:T(2,128)(2,1)} async-done(((bf16[2,1,4096]{2,0,1:T(2,128)(2,1)}), bf16[2,64,4096]{2,0,1:T(2,128)(2,1)}) %all-gather.2.cloned.1.call-update) | async-done | bytes 1048592 | tf_op jit(solution)/shard_map/all_gather | solution.py:73
  104.3 9.9 constant_dynamic-slice_fusion.2
  119.5 7.3 constant_dynamic-slice_fusion
  133.8 169.5 %all-reduce.6.cloned.1.call-done = f32[64,4096]{1,0:T(8,128)} async-done(((f32[64,4096]{1,0:T(8,128)}), f32[64,4096]{1,0:T(8,128)}) %all-reduce.6.cloned.1.call-update) | async-done | bytes 1048592 | tf_op jit(solution)/shard_map/psum | solution.py:105
  306.3 3.3 fusion.48
  317.4 5.5 collective-permute-done
  331.0 4.6 convolution_add_fusion.5
  335.6 177.1 %all-reduce.8.cloned.1.call-done = f32[64,4096]{1,0:T(8,128)} async-done(((f32[64,4096]{1,0:T(8,128)}), f32[64,4096]{1,0:T(8,128)}) %all-reduce.8.cloned.1.call-update) | async-done | bytes 1048592 | tf_op jit(solution)/shard_map/psum | solution.py:105
  512.7 3.3 fusion.58
  526.0 5.8 collective-permute-done.1
  539.1 4.6 convolution_add_fusion.4
  543.7 178.4 %all-reduce.10.cloned.1.call-done = f32[64,4096]{1,0:T(8,128)} async-done(((f32[64,4096]{1,0:T(8,128)}), f32[64,4096]{1,0:T(8,128)}) %all-reduce.10.cloned.1.call-update) | async-done | bytes 1048592 | tf_op jit(solution)/shard_map/psum | solution.py:105
  722.1 3.3 fusion.65
  725.5 3.0 fusion.62
  736.5 5.6 collective-permute-done.2
  749.7 4.7 convolution_add_fusion.3
  757.0 178.5 %all-reduce.12.cloned.1.call-done = f32[64,4096]{1,0:T(8,128)} async-done(((f32[64,4096]{1,0:T(8,128)}), f32[64,4096]{1,0:T(8,128)}) %all-reduce.12.cloned.1.call-update) | async-done | bytes 1048592 | tf_op jit(solution)/shard_map/psum | solution.py:105
  935.4 3.3 fusion.72
  947.9 6.3 collective-permute-done.3
  963.4 4.1 fusion.6
  970.4 4.1 fusion.5
  974.5 174.6 %all-reduce.14.cloned.1.call-done = f32[64,4096]{1,0:T(8,128)} async-done(((f32[64,4096]{1,0:T(8,128)}), f32[64,4096]{1,0:T(8,128)}) %all-reduce.14.cloned.1.call-update) | async-done | bytes 1048592 | tf_op jit(solution)/shard_map/psum | solution.py:105
  (218 shorter events, 103.2 us)
Async XLA Ops:
  7.2 48.1 %copy-start = (bf16[1,224,4096]{2,1,0:T(8,128)(2,1)S(1)}, bf16[1,224,4096]{2,1,0:T(8,128)(2,1)}, u32[]{:S(2)}) copy-start(bf16[1,224,4096]{2,1,0:T(8,128)(2,1)} %param.9) | copy-start | bytes 5505028
  7.2 15.0 %copy-start.71 = (s32[2]{0:T(128)S(1)}, s32[2]{0:T(128)}, u32[]{:S(2)}) copy-start(s32[2]{0:T(128)} %param.13) | copy-start | bytes 28
  7.2 15.0 %copy-start.63 = (bf16[2,1,4096]{2,0,1:T(2,128)(2,1)S(1)}, bf16[2,1,4096]{2,0,1:T(2,128)(2,1)}, u32[]{:S(2)}) copy-start(bf16[2,1,4096]{2,0,1:T(2,128)(2,1)} %param.8) | copy-start | bytes 49156
  7.2 45.1 %copy-start.40 = (f32[1,4096]{1,0:T(1,128)S(1)}, f32[1,4096]{1,0:T(1,128)}, u32[]{:S(2)}) copy-start(f32[1,4096]{1,0:T(1,128)} %param.12) | copy-start | bytes 49156
  10.0 41.1 %all-to-all-start = ((bf16[64,2,1,4096]{3,1,2,0:T(2,128)(2,1)}), bf16[64,2,1,4096]{3,1,2,0:T(2,128)(2,1)S(1)}, u32[]{:S(2)}, u32[]{:S(2)}) async-start(bf16[64,2,1,4096]{3,1,2,0:T(2,128)(2,1)} %stack.3), calls=%async_computation | async-start | bytes 2097152 | tf_op jit(solution)/shard_map/all_to_all | solution.py:76
  22.2 82.2 %all-gather.2.cloned.1.call-start = ((), (), s32[]{:S(2)}) async-start(), calls=%async_computation.1 | async-start | bytes 1064960 | tf_op jit(solution)/shard_map/all_gather | solution.py:73
  23.0 280.3 %all-reduce.6.cloned.1.call-start = ((), (), s32[]{:S(2)}) async-start(), calls=%async_computation.2 | async-start | bytes 2097152 | tf_op jit(solution)/shard_map/psum | solution.py:105
  56.8 257.8 %copy-start.34 = (f32[2,64,224]{2,1,0:T(8,128)}, f32[2,64,224]{2,1,0:T(8,128)S(1)}, u32[]{:S(2)}) copy-start(f32[2,64,224]{2,1,0:T(8,128)S(1)} %fusion.16) | copy-start | bytes 344068
  118.2 394.5 %all-reduce.8.cloned.1.call-start = ((), (), s32[]{:S(2)}) async-start(), calls=%async_computation.3 | async-start | bytes 2097152 | tf_op jit(solution)/shard_map/psum | solution.py:105
  131.3 172.0 %copy-start.25 = (bf16[64,1,1,4096]{3,1,2,0:T(2,128)(2,1)S(1)}, bf16[64,1,1,4096]{3,1,2,0:T(2,128)(2,1)}, u32[]{:S(2)}) copy-start(bf16[64,1,1,4096]{3,1,2,0:T(2,128)(2,1)} %get-tuple-element.35) | copy-start | bytes 1572868
  309.6 13.2 %collective-permute-start = (bf16[64,4096]{1,0:T(8,128)(2,1)S(1)}, bf16[64,4096]{1,0:T(8,128)(2,1)S(1)}, u32[]{:S(2)}, u32[]{:S(2)}) collective-permute-start(bf16[64,4096]{1,0:T(8,128)(2,1)S(1)} %fusion.48), channel_id=1, source_target_pairs={{1,0},{2,1},{3,2},{5,4},{6,5},{7,6},{9,8},{10,9},{11,10},{13,12},{... | collective-permute-start | bytes 1572872 | tf_op jit(solution)/shard_map/ppermute | solution.py:10
  327.3 394.9 %all-reduce.10.cloned.1.call-start = ((), (), s32[]{:S(2)}) async-start(), calls=%async_computation.4 | async-start | bytes 2097152 | tf_op jit(solution)/shard_map/psum | solution.py:105
  518.3 13.5 %collective-permute-start.1 = (bf16[64,4096]{1,0:T(8,128)(2,1)S(1)}, bf16[64,4096]{1,0:T(8,128)(2,1)S(1)}, u32[]{:S(2)}, u32[]{:S(2)}) collective-permute-start(bf16[64,4096]{1,0:T(8,128)(2,1)S(1)} %fusion.55), channel_id=1, source_target_pairs={{1,0},{2,1},{3,2},{5,4},{6,5},{7,6},{9,8},{10,9},{11,10},{13,12},{... | collective-permute-start | bytes 1572872 | tf_op jit(solution)/shard_map/ppermute | solution.py:10
  532.4 193.0 %copy-start.27 = (bf16[64,4096]{1,0:T(8,128)(2,1)}, bf16[64,4096]{1,0:T(8,128)(2,1)S(1)}, u32[]{:S(2)}) copy-start(bf16[64,4096]{1,0:T(8,128)(2,1)S(1)} %fusion.82) | copy-start | bytes 1572868
  536.2 399.3 %all-reduce.12.cloned.1.call-start = ((), (), s32[]{:S(2)}) async-start(), calls=%async_computation.5 | async-start | bytes 2097152 | tf_op jit(solution)/shard_map/psum | solution.py:105
  728.5 13.6 %collective-permute-start.2 = (bf16[64,4096]{1,0:T(8,128)(2,1)}, bf16[64,4096]{1,0:T(8,128)(2,1)S(1)}, u32[]{:S(2)}, u32[]{:S(2)}) collective-permute-start(bf16[64,4096]{1,0:T(8,128)(2,1)} %fusion.62), channel_id=1, source_target_pairs={{1,0},{2,1},{3,2},{5,4},{6,5},{7,6},{9,8},{10,9},{11,10},{13,12},{... | collective-permute-start | bytes 1572872 | tf_op jit(solution)/shard_map/ppermute | solution.py:10
  749.5 399.6 %all-reduce.14.cloned.1.call-start = ((), (), s32[]{:S(2)}) async-start(), calls=%async_computation.6 | async-start | bytes 2097152 | tf_op jit(solution)/shard_map/psum | solution.py:105
  940.5 13.7 %collective-permute-start.3 = (bf16[64,4096]{1,0:T(8,128)(2,1)}, bf16[64,4096]{1,0:T(8,128)(2,1)}, u32[]{:S(2)}, u32[]{:S(2)}) collective-permute-start(bf16[64,4096]{1,0:T(8,128)(2,1)} %fusion.69), channel_id=1, source_target_pairs={{1,0},{2,1},{3,2},{5,4},{6,5},{7,6},{9,8},{10,9},{11,10},{13,12},{... | collective-permute-start | bytes 1572872 | tf_op jit(solution)/shard_map/ppermute | solution.py:10
  970.4 178.7 %copy-start.21 = (bf16[64,1,1,4096]{3,1,2,0:T(2,128)(2,1)S(1)}, bf16[64,1,1,4096]{3,1,2,0:T(2,128)(2,1)}, u32[]{:S(2)}) copy-start(bf16[64,1,1,4096]{3,1,2,0:T(2,128)(2,1)} %copy-done.20) | copy-start | bytes 1572868
  974.4 177.5 %copy-start.46 = (bf16[2,1,4096]{2,0,1:T(2,128)(2,1)S(1)}, bf16[2,1,4096]{2,0,1:T(2,128)(2,1)}, u32[]{:S(2)}) copy-start(bf16[2,1,4096]{2,0,1:T(2,128)(2,1)} %dynamic_update_slice.20) | copy-start | bytes 49156
  974.4 180.6 %copy-start.59 = (f32[4096]{0:T(1024)S(1)}, f32[4096]{0:T(1024)}, u32[]{:S(2)}) copy-start(f32[4096]{0:T(1024)} %get-tuple-element.7) | copy-start | bytes 49156
  974.4 180.6 %copy-start.60 = (f32[4096]{0:T(1024)S(1)}, f32[4096]{0:T(1024)}, u32[]{:S(2)}) copy-start(f32[4096]{0:T(1024)} %get-tuple-element.5) | copy-start | bytes 49156
  974.4 180.6 %copy-start.61 = (f32[4096]{0:T(1024)S(1)}, f32[4096]{0:T(1024)}, u32[]{:S(2)}) copy-start(f32[4096]{0:T(1024)} %get-tuple-element.9) | copy-start | bytes 49156
  974.4 180.6 %copy-start.62 = (f32[4096]{0:T(1024)S(1)}, f32[4096]{0:T(1024)}, u32[]{:S(2)}) copy-start(f32[4096]{0:T(1024)} %get-tuple-element.11) | copy-start | bytes 49156
  (59 other events, 240.5 us)
Sparse Core Ops, SparseCore 0:
  26.3 77.9 all-gather.1
  118.3 184.9 all-reduce.5
  327.4 185.2 all-reduce.7
  536.3 185.7 all-reduce.9
  749.6 185.7 all-reduce.11
  963.5 185.5 all-reduce.13
